TPU v7x, 256 devices: a whole 4x4x8 slice. The times are simulated.
256 devices in a mesh: dp: 32 (over y, x, core), mp: 8 (over z).
Axes of the slice: x: 4, y: 4, z: 8, core: 2. Of those that a mesh axis runs over, the one named last changes fastest.
Arguments:
- activations: bfloat16 [4096, 2560], P('dp'), may hold values from -6 to 6
- grad_hidden: bfloat16 [4096, 8192], P('dp', 'mp'), may hold values from -0.059814453 to 0.059814453
- up_weight: bfloat16 [2560, 8192], P('dp', 'mp'), may hold values from -6 to 6
- error_feedback: bfloat16 [32, 2560, 8192], P('dp', None, 'mp'), may hold values from -0.75 to 0.75
- query_previous: float32 [8192, 128], P('mp'), may hold values from -6 to 6
Outputs:
- grad_input: bfloat16 [4096, 2560], P('dp', 'mp')
- error_next: bfloat16 [32, 2560, 8192], P('dp', None, 'mp')
- update: float32 [2560, 8192], P('dp', 'mp')
- query_next: float32 [8192, 128], P('mp')
All inputs are finite; a program needn't handle non-finite values.
Results may differ from a plain program's by a relative error of at most 0.0005.
Values may be sent and summed in bfloat16 or wider, within the bound.
No kernel may reach another device: no remote copies, remote signals or barrier semaphores. Data moves between devices by JAX's collectives and lax.ppermute only.
A program may use at most 128 MiB of HBM per device.

v0:
```python
import jax
import jax.numpy as jnp
from jax import lax
from jax.sharding import PartitionSpec as P

HIGHEST = lax.Precision.HIGHEST


def orthonormal(project, gram_matrix):
    factor = jnp.linalg.cholesky(gram_matrix)
    return lax.linalg.triangular_solve(
        factor, project, left_side=False, lower=True, transpose_a=True
    )


def local(activations, grad_hidden, up_weight, error_feedback, query_previous):
    replicas = lax.axis_size("dp")
    partial_input = lax.dot_general(
        grad_hidden,
        lax.all_gather(up_weight, "dp", axis=0, tiled=True),
        (((1,), (1,)), ((), ())),
        preferred_element_type=jnp.float32,
    )
    grad_input = lax.psum_scatter(partial_input, "mp", scatter_dimension=1, tiled=True).astype(
        jnp.bfloat16
    )
    local_grad = lax.dot_general(
        activations, grad_hidden, (((0,), (0,)), ((), ())), preferred_element_type=jnp.float32
    )
    merged = error_feedback[0].astype(jnp.float32) + local_grad
    project = jnp.dot(merged, query_previous, precision=HIGHEST, preferred_element_type=jnp.float32)
    project = lax.psum(project, ("dp", "mp"))
    gram_matrix = jnp.dot(project.T, project, precision=HIGHEST, preferred_element_type=jnp.float32)
    basis_full = orthonormal(project, gram_matrix)
    query_term = lax.dot_general(
        merged,
        basis_full,
        (((0,), (0,)), ((), ())),
        precision=HIGHEST,
        preferred_element_type=jnp.float32,
    )
    query_next = lax.psum(query_term, "dp") / replicas
    low_rank = lax.dot_general(
        basis_full,
        query_next,
        (((1,), (1,)), ((), ())),
        precision=HIGHEST,
        preferred_element_type=jnp.float32,
    )
    error_next = (merged - low_rank).astype(jnp.bfloat16)[None]
    row_share = merged.shape[0] // replicas
    update = lax.dynamic_slice_in_dim(low_rank, lax.axis_index("dp") * row_share, row_share, 0)
    return (grad_input, error_next, update, query_next)


def solution(mesh):
    in_specs = (P("dp", None), P("dp", "mp"), P("dp", "mp"), P("dp", None, "mp"), P("mp", None))
    out_specs = (P("dp", "mp"), P("dp", None, "mp"), P("dp", "mp"), P("mp", None))
    return jax.shard_map(local, mesh=mesh, in_specs=in_specs, out_specs=out_specs, check_vma=False)
```

profile of v0, /device:TPU:4, one launch (start us, length us, event | category | flops | bytes accessed | tf_op | source)
XLA Modules:
  0.0 501.2 jit_solution(10728935111397148013)
XLA Ops:
  8.0 0.0 copy-start
  8.0 0.0 all-reduce.3.cloned.1.call-start
  8.1 1.0 copy-done
  9.1 0.0 copy-start.5
  9.1 4.2 convert_add_fusion
  13.3 0.0 copy-start.1
  13.3 4.0 copy-done.1
  17.2 0.0 copy-done.5
  17.2 9.4 %fusion.6 = f32[2560,128]{1,0:T(8,128)} fusion(f32[2560,1024]{1,0:T(8,128)S(1)} %convert_add_fusion, f32[1024,128]{1,0:T(8,128)S(1)} %copy-done.5), kind=kOutput, calls=%fused_computation.16 | convolution fusion | flops 4026531840 | bytes 12320768 | tf_op jit(solution)/shard_map/dot_general | solution.py:31
  26.7 0.0 all-reduce.3.cloned.1.call-update
  26.7 0.0 all-gather.2.cloned.1.call-start
  26.7 0.5 all-gather.2.cloned.1.call-update
  27.3 0.5 all-reduce.5.cloned.1.call-start
  27.8 261.2 %all-reduce.3.cloned.1.call-done = f32[2560,128]{1,0:T(8,128)} async-done(((f32[2560,128]{1,0:T(8,128)}), f32[2560,128]{1,0:T(8,128)}) %all-reduce.3.cloned.1.call-update) | async-done | bytes 1310736 | tf_op jit(solution)/shard_map/psum | solution.py:32
  288.9 3.9 fusion.7
  292.9 0.1 copy.9
  293.0 11.7 %cholesky.16 = f32[128,128]{1,0:T(8,128)S(1)} custom-call(f32[128,128]{1,0:T(8,128)S(1)} %fusion.4), custom_call_target="Cholesky" | custom-call | tf_op jit(solution)/shard_map/jit(cholesky)/cholesky | solution.py:10
  304.7 0.6 compare_reduce_fusion
  305.4 0.7 fusion.1
  306.0 9.8 %custom-call.6 = f32[1,128,128]{1,2,0:T(8,128)S(1)} custom-call(f32[1,128,128]{2,1,0:T(8,128)S(1)} %fusion.1), custom_call_target="InvertDiagBlocksLowerTriangular" | custom-call | tf_op jit(solution)/shard_map/triangular_solve | solution.py:11
  315.9 2.5 fusion.2
  318.4 0.0 copy-start.4
  318.4 19.9 %fusion.8 = f32[1024,128]{1,0:T(8,128)} fusion(f32[2560,1024]{1,0:T(8,128)} %copy-done.1, f32[2560,128]{1,0:T(8,128)S(1)} %fusion.2), kind=kOutput, calls=%fused_computation.18 | convolution fusion | flops 4026531840 | bytes 12320768 | tf_op jit(solution)/shard_map/dot_general | solution.py:35
  338.3 0.0 all-reduce.5.cloned.1.call-update
  338.3 0.3 reduce-scatter.2.cloned.1.call-start
  338.6 0.0 all-gather.2.cloned.1.call-done
  338.6 0.0 copy-done.4
  338.6 5.1 %fusion.5 = f32[128,2560]{0,1:T(8,128)} fusion(bf16[128,1024]{1,0:T(8,128)(2,1)S(1)} %copy-done.4, bf16[2560,1024]{1,0:T(8,128)(2,1)} %all-gather.2.cloned.1.call-done), kind=kOutput, calls=%fused_computation.15 | convolution fusion | flops 671088640 | bytes 6815744 | tf_op jit(solution)/shard_map/dot_general | solution.py:18
  343.7 0.0 reduce-scatter.2.cloned.1.call-update
  343.7 106.1 %all-reduce.5.cloned.1.call-done = f32[1024,128]{1,0:T(8,128)} async-done(((f32[1024,128]{1,0:T(8,128)}), f32[1024,128]{1,0:T(8,128)}) %all-reduce.5.cloned.1.call-update) | async-done | bytes 524304 | tf_op jit(solution)/shard_map/psum | solution.py:42
  449.8 1.1 broadcast_multiply_fusion
  450.9 0.0 copy-start.3
  450.9 8.4 %fusion.9 = f32[2560,1024]{1,0:T(8,128)S(1)} fusion(f32[2560,128]{1,0:T(8,128)S(1)} %fusion.2, f32[1024,128]{1,0:T(8,128)S(1)} %broadcast_multiply_fusion), kind=kOutput, calls=%fused_computation.19 | convolution fusion | flops 4026531840 | bytes 12320768 | tf_op jit(solution)/shard_map/dot_general | solution.py:43
  459.4 0.0 copy-done.3
  459.4 0.0 copy-start.2
  459.4 3.8 copy-done.2
  463.2 0.7 constant_dynamic-slice_fusion
  464.0 11.5 %fusion = bf16[1,2560,1024]{2,1,0:T(8,128)(2,1)} fusion(f32[2560,1024]{1,0:T(8,128)} %copy-done.1, f32[2560,1024]{1,0:T(8,128)} %copy-done.2), kind=kLoop, calls=%fused_computation.2 | loop fusion | flops 5242880 | bytes 26214400 | tf_op jit(solution)/shard_map/broadcast_in_dim | solution.py:50
  475.5 16.3 %reduce-scatter.2.cloned.1.call-done = f32[128,320]{0,1:T(8,128)} async-done(((f32[128,2560]{0,1:T(8,128)}), f32[128,320]{0,1:T(8,128)}) %reduce-scatter.2.cloned.1.call-update) | async-done | bytes 163856 | tf_op jit(solution)/shard_map/reduce_scatter | solution.py:24
  491.8 1.6 convert_element_type.12
  (2 shorter events, 0.0 us)
Async XLA Ops:
  8.0 1.1 copy-start
  8.0 280.9 %all-reduce.3.cloned.1.call-start = ((), (), s32[]{:S(2)}) async-start(), calls=%async_computation.3 | async-start | bytes 2621440 | tf_op jit(solution)/shard_map/psum | solution.py:32
  9.1 8.2 %copy-start.5 = (f32[1024,128]{1,0:T(8,128)S(1)}, f32[1024,128]{1,0:T(8,128)}, u32[]{:S(2)}) copy-start(f32[1024,128]{1,0:T(8,128)} %param.9) | copy-start | bytes 1572868
  13.3 4.0 copy-start.1
  26.7 311.9 %all-gather.2.cloned.1.call-start = ((), (), s32[]{:S(2)}) async-start(), calls=%async_computation.1 | async-start | bytes 5406720 | tf_op jit(solution)/shard_map/all_gather | solution.py:20
  27.3 422.5 %all-reduce.5.cloned.1.call-start = ((), (), s32[]{:S(2)}) async-start(), calls=%async_computation.4 | async-start | bytes 1048576 | tf_op jit(solution)/shard_map/psum | solution.py:42
  318.4 20.3 %copy-start.4 = (bf16[128,1024]{1,0:T(8,128)(2,1)S(1)}, bf16[128,1024]{1,0:T(8,128)(2,1)}, u32[]{:S(2)}) copy-start(bf16[128,1024]{1,0:T(8,128)(2,1)} %param.6) | copy-start | bytes 786436
  338.3 153.5 %reduce-scatter.2.cloned.1.call-start = ((), (), s32[]{:S(2)}) async-start(), calls=%async_computation.2 | async-start | bytes 1474560 | tf_op jit(solution)/shard_map/reduce_scatter | solution.py:24
  450.9 8.5 %copy-start.3 = (f32[1024,128]{1,0:T(8,128)}, f32[1024,128]{1,0:T(8,128)S(1)}, u32[]{:S(2)}) copy-start(f32[1024,128]{1,0:T(8,128)S(1)} %broadcast_multiply_fusion) | copy-start | bytes 1572868
  459.4 3.8 copy-start.2
Sparse Core Ops, SparseCore 0:
  26.8 262.0 all-reduce.2
Sparse Core Ops, SparseCore 1:
  29.7 54.2 all-gather.1
  338.4 111.3 all-reduce.4
  452.2 39.5 reduce-scatter.1
where the time goes:
time: 509 us; the launch traced here: 501 us
  waiting for transfers between devices  384 us (75%)
  matrix products  53.5 us (11%)
  other arithmetic  37 us (7%)
  between operations  16 us (3%)
  local copies, waits for them, and re-layouts  9.68 us (2%)
    psum x1, waiting for transfers between devices, local(): project = lax.psum(project, ('dp', 'mp'))  261 us
    psum x1, waiting for transfers between devices, local(): query_next = lax.psum(query_term, 'dp') / replicas  106 us
    dot_general x1, matrix products, local(): lax.dot_general(merged, basis_full, (((0,), (0,)), ((), ())), precision=H...  19.9 us
    reduce_scatter x1, waiting for transfers between devices, local(): lax.psum_scatter(partial_input, 'mp', scatter_dimension=1, tiled=True)  16.3 us
    another operation x3, other arithmetic, orthonormal(): factor = jnp.linalg.cholesky(gram_matrix)  12.4 us
    broadcast_in_dim x1, other arithmetic, local(): error_next = (merged - low_rank).astype(jnp.bfloat16)[None]  11.5 us
    another operation x2, other arithmetic, orthonormal(): lax.linalg.triangular_solve(factor, project, left_side=False, lower=True,...  10.5 us
  transfers between devices with their start and end apart: 4, of which 3 were waited for; matrix products, arithmetic and copies ran while one was open for 15% of the time, Pallas kernels for 0%

commit v1 on v0

--- a/solution.py
+++ b/solution.py
@@ -29,7 +29,8 @@
     )
     merged = error_feedback[0].astype(jnp.float32) + local_grad
     project = jnp.dot(merged, query_previous, precision=HIGHEST, preferred_element_type=jnp.float32)
-    project = lax.psum(project, ("dp", "mp"))
+    one_axis = lax.psum(project, "mp")
+    project = lax.psum(one_axis, "dp")
     gram_matrix = jnp.dot(project.T, project, precision=HIGHEST, preferred_element_type=jnp.float32)
     basis_full = orthonormal(project, gram_matrix)
     query_term = lax.dot_general(

time: 509 us -> 452 us (0.89)
  waiting for transfers between devices: 384 us -> 329 us
    psum x1 -> x2, waiting for transfers between devices: 261 us -> 195 us  [the longest x1 115 us: local(): project = lax.psum(one_axis, 'dp')]
    psum x1, waiting for transfers between devices: 106 us -> 112 us  [local(): query_next = lax.psum(query_term, 'dp') / replicas]
  transfers between devices with their start and end apart: 4 -> 5, of which waited for: 3 -> 5; matrix products, arithmetic and copies ran while one was open for 15% -> 17% of each run, Pallas kernels for 0% -> 0%
where the time goes in v1:
time: 452 us; the launch traced here: 445 us
  waiting for transfers between devices  329 us (73%)
  matrix products  53.5 us (12%)
  other arithmetic  37.1 us (8%)
  between operations  14.1 us (3%)
  local copies, waits for them, and re-layouts  9.68 us (2%)
    psum x1, waiting for transfers between devices, local(): project = lax.psum(one_axis, 'dp')  115 us
    psum x1, waiting for transfers between devices, local(): query_next = lax.psum(query_term, 'dp') / replicas  112 us
    psum x1, waiting for transfers between devices, local(): one_axis = lax.psum(project, 'mp')  80.2 us
    dot_general x1, matrix products, local(): lax.dot_general(merged, basis_full, (((0,), (0,)), ((), ())), precision=H...  19.9 us
    reduce_scatter x1, waiting for transfers between devices, local(): lax.psum_scatter(partial_input, 'mp', scatter_dimension=1, tiled=True)  16.4 us
    another operation x3, other arithmetic, orthonormal(): factor = jnp.linalg.cholesky(gram_matrix)  12.4 us
    broadcast_in_dim x1, other arithmetic, local(): error_next = (merged - low_rank).astype(jnp.bfloat16)[None]  11.6 us
    another operation x2, other arithmetic, orthonormal(): lax.linalg.triangular_solve(factor, project, left_side=False, lower=True,...  10.5 us
  transfers between devices with their start and end apart: 5, of which 5 were waited for; matrix products, arithmetic and copies ran while one was open for 17% of the time, Pallas kernels for 0%

profile of v1, /device:TPU:4, one launch (start us, length us, event | category | flops | bytes accessed | tf_op | source)
XLA Modules:
  0.0 444.7 jit_solution(10955744295953823353)
XLA Ops:
  7.2 0.0 copy-start
  7.2 0.0 all-reduce.4.cloned.1.call-start
  7.2 1.0 copy-done
  8.3 0.0 copy-start.5
  8.3 4.2 convert_add_fusion
  12.4 0.0 copy-start.1
  12.5 4.0 copy-done.1
  16.4 0.0 copy-done.5
  16.4 9.4 %fusion.6 = f32[2560,128]{1,0:T(8,128)} fusion(f32[2560,1024]{1,0:T(8,128)S(1)} %convert_add_fusion, f32[1024,128]{1,0:T(8,128)S(1)} %copy-done.5), kind=kOutput, calls=%fused_computation.16 | convolution fusion | flops 4026531840 | bytes 12320768 | tf_op jit(solution)/shard_map/dot_general | solution.py:31
  25.8 0.0 all-reduce.4.cloned.1.call-update
  25.9 0.0 all-reduce.6.cloned.1.call-start
  25.9 80.2 %all-reduce.4.cloned.1.call-done = f32[2560,128]{1,0:T(8,128)} async-done(((f32[2560,128]{1,0:T(8,128)}), f32[2560,128]{1,0:T(8,128)}) %all-reduce.4.cloned.1.call-update) | async-done | bytes 1310736 | tf_op jit(solution)/shard_map/psum | solution.py:32
  106.1 0.0 all-reduce.6.cloned.1.call-update
  106.2 0.0 all-gather.2.cloned.1.call-start
  106.2 0.7 all-gather.2.cloned.1.call-update
  106.9 0.5 all-reduce.8.cloned.1.call-start
  107.4 115.3 %all-reduce.6.cloned.1.call-done = f32[2560,128]{1,0:T(8,128)} async-done(((f32[2560,128]{1,0:T(8,128)}), f32[2560,128]{1,0:T(8,128)}) %all-reduce.6.cloned.1.call-update) | async-done | bytes 1310736 | tf_op jit(solution)/shard_map/psum | solution.py:33
  222.7 3.9 fusion.7
  226.6 0.1 copy.9
  226.7 11.7 %cholesky.16 = f32[128,128]{1,0:T(8,128)S(1)} custom-call(f32[128,128]{1,0:T(8,128)S(1)} %fusion.4), custom_call_target="Cholesky" | custom-call | tf_op jit(solution)/shard_map/jit(cholesky)/cholesky | solution.py:10
  238.5 0.6 compare_reduce_fusion
  239.1 0.7 fusion.1
  239.8 9.8 %custom-call.6 = f32[1,128,128]{1,2,0:T(8,128)S(1)} custom-call(f32[1,128,128]{2,1,0:T(8,128)S(1)} %fusion.1), custom_call_target="InvertDiagBlocksLowerTriangular" | custom-call | tf_op jit(solution)/shard_map/triangular_solve | solution.py:11
  249.6 2.5 fusion.2
  252.1 0.0 copy-start.4
  252.1 19.9 %fusion.8 = f32[1024,128]{1,0:T(8,128)} fusion(f32[2560,1024]{1,0:T(8,128)} %copy-done.1, f32[2560,128]{1,0:T(8,128)S(1)} %fusion.2), kind=kOutput, calls=%fused_computation.18 | convolution fusion | flops 4026531840 | bytes 12320768 | tf_op jit(solution)/shard_map/dot_general | solution.py:36
  272.0 0.0 all-reduce.8.cloned.1.call-update
  272.1 0.3 reduce-scatter.2.cloned.1.call-start
  272.3 4.8 %all-gather.2.cloned.1.call-done = bf16[2560,1024]{1,0:T(8,128)(2,1)} async-done(((bf16[80,1024]{1,0:T(8,128)(2,1)}), bf16[2560,1024]{1,0:T(8,128)(2,1)}) %all-gather.2.cloned.1.call-update) | async-done | bytes 5242896 | tf_op jit(solution)/shard_map/all_gather | solution.py:20
  277.1 0.0 copy-done.4
  277.1 5.1 %fusion.5 = f32[128,2560]{0,1:T(8,128)} fusion(bf16[128,1024]{1,0:T(8,128)(2,1)S(1)} %copy-done.4, bf16[2560,1024]{1,0:T(8,128)(2,1)} %all-gather.2.cloned.1.call-done), kind=kOutput, calls=%fused_computation.15 | convolution fusion | flops 671088640 | bytes 6815744 | tf_op jit(solution)/shard_map/dot_general | solution.py:18
  282.2 0.0 reduce-scatter.2.cloned.1.call-update
  282.2 112.1 %all-reduce.8.cloned.1.call-done = f32[1024,128]{1,0:T(8,128)} async-done(((f32[1024,128]{1,0:T(8,128)}), f32[1024,128]{1,0:T(8,128)}) %all-reduce.8.cloned.1.call-update) | async-done | bytes 524304 | tf_op jit(solution)/shard_map/psum | solution.py:43
  394.3 1.1 broadcast_multiply_fusion
  395.4 0.0 copy-start.3
  395.4 8.4 %fusion.9 = f32[2560,1024]{1,0:T(8,128)S(1)} fusion(f32[2560,128]{1,0:T(8,128)S(1)} %fusion.2, f32[1024,128]{1,0:T(8,128)S(1)} %broadcast_multiply_fusion), kind=kOutput, calls=%fused_computation.19 | convolution fusion | flops 4026531840 | bytes 12320768 | tf_op jit(solution)/shard_map/dot_general | solution.py:44
  403.9 0.0 copy-done.3
  403.9 0.0 copy-start.2
  403.9 3.8 copy-done.2
  407.7 0.7 constant_dynamic-slice_fusion
  408.5 11.6 %fusion = bf16[1,2560,1024]{2,1,0:T(8,128)(2,1)} fusion(f32[2560,1024]{1,0:T(8,128)} %copy-done.1, f32[2560,1024]{1,0:T(8,128)} %copy-done.2), kind=kLoop, calls=%fused_computation.2 | loop fusion | flops 5242880 | bytes 26214400 | tf_op jit(solution)/shard_map/broadcast_in_dim | solution.py:51
  420.0 16.4 %reduce-scatter.2.cloned.1.call-done = f32[128,320]{0,1:T(8,128)} async-done(((f32[128,2560]{0,1:T(8,128)}), f32[128,320]{0,1:T(8,128)}) %reduce-scatter.2.cloned.1.call-update) | async-done | bytes 163856 | tf_op jit(solution)/shard_map/reduce_scatter | solution.py:24
  436.4 1.6 convert_element_type.12
  (2 shorter events, 0.0 us)
Async XLA Ops:
  7.2 1.1 copy-start
  7.2 99.0 %all-reduce.4.cloned.1.call-start = ((), (), s32[]{:S(2)}) async-start(), calls=%async_computation.3 | async-start | bytes 2621440 | tf_op jit(solution)/shard_map/psum | solution.py:32
  8.3 8.2 %copy-start.5 = (f32[1024,128]{1,0:T(8,128)S(1)}, f32[1024,128]{1,0:T(8,128)}, u32[]{:S(2)}) copy-start(f32[1024,128]{1,0:T(8,128)} %param.9) | copy-start | bytes 1572868
  12.4 4.0 copy-start.1
  25.9 196.8 %all-reduce.6.cloned.1.call-start = ((), (), s32[]{:S(2)}) async-start(), calls=%async_computation.4 | async-start | bytes 2621440 | tf_op jit(solution)/shard_map/psum | solution.py:33
  106.2 170.9 %all-gather.2.cloned.1.call-start = ((), (), s32[]{:S(2)}) async-start(), calls=%async_computation.1 | async-start | bytes 5406720 | tf_op jit(solution)/shard_map/all_gather | solution.py:20
  106.9 287.4 %all-reduce.8.cloned.1.call-start = ((), (), s32[]{:S(2)}) async-start(), calls=%async_computation.5 | async-start | bytes 1048576 | tf_op jit(solution)/shard_map/psum | solution.py:43
  252.1 25.0 %copy-start.4 = (bf16[128,1024]{1,0:T(8,128)(2,1)S(1)}, bf16[128,1024]{1,0:T(8,128)(2,1)}, u32[]{:S(2)}) copy-start(bf16[128,1024]{1,0:T(8,128)(2,1)} %param.6) | copy-start | bytes 786436
  272.1 164.3 %reduce-scatter.2.cloned.1.call-start = ((), (), s32[]{:S(2)}) async-start(), calls=%async_computation.2 | async-start | bytes 1474560 | tf_op jit(solution)/shard_map/reduce_scatter | solution.py:24
  395.4 8.5 %copy-start.3 = (f32[1024,128]{1,0:T(8,128)}, f32[1024,128]{1,0:T(8,128)S(1)}, u32[]{:S(2)}) copy-start(f32[1024,128]{1,0:T(8,128)S(1)} %broadcast_multiply_fusion) | copy-start | bytes 1572868
  403.9 3.8 copy-start.2
Sparse Core Ops, SparseCore 0:
  26.0 80.1 all-reduce.3
  109.4 113.1 all-reduce.5
  225.2 51.8 all-gather.1
  280.7 113.5 all-reduce.7
  396.9 39.4 reduce-scatter.1
